TPU v7x, 32 devices: a whole 2x2x4 slice. The times are simulated.
32 devices in a mesh: sx: 4 (over y, x), sy: 2 (over core), op: 4 (over z).
Axes of the slice: x: 2, y: 2, z: 4, core: 2. Of those that a mesh axis runs over, the one named last changes fastest.
Arguments:
- op_real: float32 [4, 2, 6144, 6144], P('sx', 'sy', 'op'), may hold values from -0.0546875 to 0.0546875
- op_imag: float32 [4, 2, 6144, 6144], P('sx', 'sy', 'op'), may hold values from -0.0546875 to 0.0546875
- coef_right: float32 [4, 2, 2, 6144], P('sx', 'sy', None, 'op'), may hold values from -3 to 3
- coef_upper: float32 [4, 2, 2, 6144], P('sx', 'sy', None, 'op'), may hold values from -3 to 3
- sources: float32 [4, 2, 2, 16, 6144], P('sx', 'sy', None, None, 'op'), may hold values from -6 to 6
Outputs:
- traces: float32 [4, 2, 2, 16, 6144], P('sx', 'sy', None, None, 'op')
All inputs are finite; a program needn't handle non-finite values.
Results may differ from a plain program's by a relative error of at most 0.0003.
Values sent between devices are 32-bit elements; how exact they have to be, the bound alone decides.
A program may use at most 128 MiB of HBM per device.

v0:
```python
import jax
import jax.numpy as jnp
from jax import lax
from jax.sharding import PartitionSpec as P

NB = 2


def from_behind(value, axis, by):
    size = lax.axis_size(axis)
    pairs = [(i, i + by) for i in range(size) if 0 <= i + by < size]
    return lax.ppermute(value, axis, pairs)


def contract(left, right):
    return lax.dot_general(
        left,
        right,
        (((1,), (1,)), ((), ())),
        precision=lax.Precision.HIGHEST,
        preferred_element_type=jnp.float32,
    )


def complex_scale(coef, field):
    real_part = coef[0][None, :] * field[0] - coef[1][None, :] * field[1]
    imag_part = coef[0][None, :] * field[1] + coef[1][None, :] * field[0]
    return jnp.stack([real_part, imag_part])


def shards(op_real, op_imag, coef_right, coef_upper, sources):
    real_rows = op_real[0, 0]
    imag_rows = op_imag[0, 0]
    right_coef = coef_right[0, 0]
    upper_coef = coef_upper[0, 0]
    fields = sources[0, 0]
    local_rows = real_rows.shape[0]
    batch_width = fields.shape[1] // NB
    diagonal_index = lax.axis_index("sx") + lax.axis_index("sy")
    diagonals = lax.axis_size("sx") + lax.axis_size("sy") - 1

    def accumulate(portion):
        columns = portion.shape[2]
        stacked = portion.reshape(2 * batch_width, columns)
        with_real = contract(stacked, real_rows)
        with_imag = contract(stacked, imag_rows)
        real_part = with_real[:batch_width] - with_imag[batch_width:]
        imag_part = with_imag[:batch_width] + with_real[batch_width:]
        return jnp.stack([real_part, imag_part])

    def section(which, active, state, outputs):
        from_left = from_behind(state, "sx", 1)
        from_below = from_behind(state, "sy", 1)
        offset = (jnp.clip(which, 0, NB - 1) * batch_width).astype(jnp.int32)
        source_block = lax.dynamic_slice_in_dim(fields, offset, batch_width, 1)
        incoming = (
            source_block
            + complex_scale(right_coef, from_left)
            + complex_scale(upper_coef, from_below)
        )
        result = accumulate(lax.all_gather(incoming, "op", axis=2, tiled=True))
        new_state = jnp.where(active, result, state)
        current = lax.dynamic_slice_in_dim(outputs, offset, batch_width, 1)
        written = lax.dynamic_update_slice_in_dim(
            outputs, jnp.where(active, result, current), offset, 1
        )
        return (new_state, written)

    state0 = jnp.zeros((2, batch_width, local_rows), jnp.float32)
    outputs0 = jnp.zeros(fields.shape, jnp.float32)

    def turn_natural(section_no, carry):
        which = section_no // diagonals
        active = diagonal_index == section_no % diagonals
        return section(which, active, carry[0], carry[1])

    final_state, outputs = lax.fori_loop(0, NB * diagonals, turn_natural, (state0, outputs0))
    return outputs[None, None]


def solution(mesh):
    return jax.shard_map(
        shards,
        mesh=mesh,
        in_specs=(
            P("sx", "sy", "op", None),
            P("sx", "sy", "op", None),
            P("sx", "sy", None, "op"),
            P("sx", "sy", None, "op"),
            P("sx", "sy", None, None, "op"),
        ),
        out_specs=P("sx", "sy", None, None, "op"),
        check_vma=False,
    )
```

profile of v0, /device:TPU:7, one launch (start us, length us, event | category | flops | bytes accessed | tf_op | source)
XLA Modules:
  0.0 921.5 jit_solution(2045879174206269750)
XLA Ops:
  0.0 920.7 %while.18 = (s32[]{:T(128)}, f32[2,8,1536]{2,1,0:T(8,128)S(1)}, f32[2,16,1536]{2,1,0:T(8,128)S(1)}, s32[]{:T(128)}, f32[2,16,1536]{2,1,0:T(8,128)}, /*index=5*/f...) while((s32[]{:T(128)}, f32[2,8,1536]{2,1,0:T(8,128)S(1)}, ...), condition=%wide.region_1.2_spmd.clone, body=%wide.region_0.1_spmd.clone.sunk | while | flops 3624271872 | bytes 79602096 | solution.py:77
  0.1 1.3 collective-permute-start.1
  1.4 1.3 collective-permute-start
  3.6 3.1 collective-permute-done
  6.7 0.9 fusion.22
  7.7 11.6 %all_gather.12 = f32[2,8,6144]{2,1,0:T(8,128)S(1)} all-gather(f32[2,8,1536]{2,1,0:T(8,128)S(1)} %fusion.22), channel_id=1, replica_groups=mesh['sx'=4,'sy'=2,'op'=4] {'op'}, dimensions={2}, use_global_device_ids=true | all-gather | bytes 491520 | tf_op jit(solution)/shard_map/while/body/eval_jaxpr/all_gather | solution.py:61
  19.2 34.4 %fusion.24 = f32[16,1536]{1,0:T(8,128)S(1)} fusion(f32[1536,6144]{1,0:T(8,128)} %get-tuple-element.407, f32[2,8,6144]{2,1,0:T(8,128)S(1)} %all_gather.12), kind=kOutput, calls=%fused_computation.2.clone.1 | convolution fusion | flops 1811939328 | bytes 38240256 | tf_op jit(solution)/shard_map/while/body/eval_jaxpr/dot_general | solution.py:16
  53.6 34.6 %fusion.23 = f32[16,1536]{1,0:T(8,128)S(1)} fusion(f32[1536,6144]{1,0:T(8,128)} %get-tuple-element.408, f32[2,8,6144]{2,1,0:T(8,128)S(1)} %all_gather.12), kind=kOutput, calls=%fused_computation.clone.1 | convolution fusion | flops 1811939328 | bytes 38240256 | tf_op jit(solution)/shard_map/while/body/eval_jaxpr/dot_general | solution.py:16
  88.3 1.3 collective-permute-start.1
  89.6 1.3 collective-permute-start
  91.8 4.0 collective-permute-done.1
  95.9 0.9 fusion.22
  96.8 12.0 %all_gather.12 = f32[2,8,6144]{2,1,0:T(8,128)S(1)} all-gather(f32[2,8,1536]{2,1,0:T(8,128)S(1)} %fusion.22), channel_id=1, replica_groups=mesh['sx'=4,'sy'=2,'op'=4] {'op'}, dimensions={2}, use_global_device_ids=true | all-gather | bytes 491520 | tf_op jit(solution)/shard_map/while/body/eval_jaxpr/all_gather | solution.py:61
  108.8 34.4 %fusion.24 = f32[16,1536]{1,0:T(8,128)S(1)} fusion(f32[1536,6144]{1,0:T(8,128)} %get-tuple-element.407, f32[2,8,6144]{2,1,0:T(8,128)S(1)} %all_gather.12), kind=kOutput, calls=%fused_computation.2.clone.1 | convolution fusion | flops 1811939328 | bytes 38240256 | tf_op jit(solution)/shard_map/while/body/eval_jaxpr/dot_general | solution.py:16
  143.2 34.6 %fusion.23 = f32[16,1536]{1,0:T(8,128)S(1)} fusion(f32[1536,6144]{1,0:T(8,128)} %get-tuple-element.408, f32[2,8,6144]{2,1,0:T(8,128)S(1)} %all_gather.12), kind=kOutput, calls=%fused_computation.clone.1 | convolution fusion | flops 1811939328 | bytes 38240256 | tf_op jit(solution)/shard_map/while/body/eval_jaxpr/dot_general | solution.py:16
  177.9 1.3 collective-permute-start.1
  179.2 1.3 collective-permute-start
  181.4 7.0 collective-permute-done.1
  189.4 12.0 %all_gather.12 = f32[2,8,6144]{2,1,0:T(8,128)S(1)} all-gather(f32[2,8,1536]{2,1,0:T(8,128)S(1)} %fusion.22), channel_id=1, replica_groups=mesh['sx'=4,'sy'=2,'op'=4] {'op'}, dimensions={2}, use_global_device_ids=true | all-gather | bytes 491520 | tf_op jit(solution)/shard_map/while/body/eval_jaxpr/all_gather | solution.py:61
  201.4 34.4 %fusion.24 = f32[16,1536]{1,0:T(8,128)S(1)} fusion(f32[1536,6144]{1,0:T(8,128)} %get-tuple-element.407, f32[2,8,6144]{2,1,0:T(8,128)S(1)} %all_gather.12), kind=kOutput, calls=%fused_computation.2.clone.1 | convolution fusion | flops 1811939328 | bytes 38240256 | tf_op jit(solution)/shard_map/while/body/eval_jaxpr/dot_general | solution.py:16
  235.8 34.6 %fusion.23 = f32[16,1536]{1,0:T(8,128)S(1)} fusion(f32[1536,6144]{1,0:T(8,128)} %get-tuple-element.408, f32[2,8,6144]{2,1,0:T(8,128)S(1)} %all_gather.12), kind=kOutput, calls=%fused_computation.clone.1 | convolution fusion | flops 1811939328 | bytes 38240256 | tf_op jit(solution)/shard_map/while/body/eval_jaxpr/dot_general | solution.py:16
  270.5 1.3 collective-permute-start.1
  271.8 1.3 collective-permute-start
  274.0 7.1 collective-permute-done.1
  281.1 0.9 fusion.22
  282.0 11.8 %all_gather.12 = f32[2,8,6144]{2,1,0:T(8,128)S(1)} all-gather(f32[2,8,1536]{2,1,0:T(8,128)S(1)} %fusion.22), channel_id=1, replica_groups=mesh['sx'=4,'sy'=2,'op'=4] {'op'}, dimensions={2}, use_global_device_ids=true | all-gather | bytes 491520 | tf_op jit(solution)/shard_map/while/body/eval_jaxpr/all_gather | solution.py:61
  293.8 34.4 %fusion.24 = f32[16,1536]{1,0:T(8,128)S(1)} fusion(f32[1536,6144]{1,0:T(8,128)} %get-tuple-element.407, f32[2,8,6144]{2,1,0:T(8,128)S(1)} %all_gather.12), kind=kOutput, calls=%fused_computation.2.clone.1 | convolution fusion | flops 1811939328 | bytes 38240256 | tf_op jit(solution)/shard_map/while/body/eval_jaxpr/dot_general | solution.py:16
  328.2 34.6 %fusion.23 = f32[16,1536]{1,0:T(8,128)S(1)} fusion(f32[1536,6144]{1,0:T(8,128)} %get-tuple-element.408, f32[2,8,6144]{2,1,0:T(8,128)S(1)} %all_gather.12), kind=kOutput, calls=%fused_computation.clone.1 | convolution fusion | flops 1811939328 | bytes 38240256 | tf_op jit(solution)/shard_map/while/body/eval_jaxpr/dot_general | solution.py:16
  362.9 1.3 collective-permute-start.1
  364.2 1.3 collective-permute-start
  366.4 7.3 collective-permute-done.1
  374.7 11.6 %all_gather.12 = f32[2,8,6144]{2,1,0:T(8,128)S(1)} all-gather(f32[2,8,1536]{2,1,0:T(8,128)S(1)} %fusion.22), channel_id=1, replica_groups=mesh['sx'=4,'sy'=2,'op'=4] {'op'}, dimensions={2}, use_global_device_ids=true | all-gather | bytes 491520 | tf_op jit(solution)/shard_map/while/body/eval_jaxpr/all_gather | solution.py:61
  386.3 34.4 %fusion.24 = f32[16,1536]{1,0:T(8,128)S(1)} fusion(f32[1536,6144]{1,0:T(8,128)} %get-tuple-element.407, f32[2,8,6144]{2,1,0:T(8,128)S(1)} %all_gather.12), kind=kOutput, calls=%fused_computation.2.clone.1 | convolution fusion | flops 1811939328 | bytes 38240256 | tf_op jit(solution)/shard_map/while/body/eval_jaxpr/dot_general | solution.py:16
  420.7 34.6 %fusion.23 = f32[16,1536]{1,0:T(8,128)S(1)} fusion(f32[1536,6144]{1,0:T(8,128)} %get-tuple-element.408, f32[2,8,6144]{2,1,0:T(8,128)S(1)} %all_gather.12), kind=kOutput, calls=%fused_computation.clone.1 | convolution fusion | flops 1811939328 | bytes 38240256 | tf_op jit(solution)/shard_map/while/body/eval_jaxpr/dot_general | solution.py:16
  455.4 1.3 collective-permute-start.1
  456.7 1.3 collective-permute-start
  458.9 7.7 collective-permute-done.1
  467.6 11.8 %all_gather.12 = f32[2,8,6144]{2,1,0:T(8,128)S(1)} all-gather(f32[2,8,1536]{2,1,0:T(8,128)S(1)} %fusion.22), channel_id=1, replica_groups=mesh['sx'=4,'sy'=2,'op'=4] {'op'}, dimensions={2}, use_global_device_ids=true | all-gather | bytes 491520 | tf_op jit(solution)/shard_map/while/body/eval_jaxpr/all_gather | solution.py:61
  479.4 34.4 %fusion.24 = f32[16,1536]{1,0:T(8,128)S(1)} fusion(f32[1536,6144]{1,0:T(8,128)} %get-tuple-element.407, f32[2,8,6144]{2,1,0:T(8,128)S(1)} %all_gather.12), kind=kOutput, calls=%fused_computation.2.clone.1 | convolution fusion | flops 1811939328 | bytes 38240256 | tf_op jit(solution)/shard_map/while/body/eval_jaxpr/dot_general | solution.py:16
  513.8 34.6 %fusion.23 = f32[16,1536]{1,0:T(8,128)S(1)} fusion(f32[1536,6144]{1,0:T(8,128)} %get-tuple-element.408, f32[2,8,6144]{2,1,0:T(8,128)S(1)} %all_gather.12), kind=kOutput, calls=%fused_computation.clone.1 | convolution fusion | flops 1811939328 | bytes 38240256 | tf_op jit(solution)/shard_map/while/body/eval_jaxpr/dot_general | solution.py:16
  548.4 1.3 collective-permute-start.1
  549.7 1.3 collective-permute-start
  551.9 7.7 collective-permute-done.1
  560.6 11.8 %all_gather.12 = f32[2,8,6144]{2,1,0:T(8,128)S(1)} all-gather(f32[2,8,1536]{2,1,0:T(8,128)S(1)} %fusion.22), channel_id=1, replica_groups=mesh['sx'=4,'sy'=2,'op'=4] {'op'}, dimensions={2}, use_global_device_ids=true | all-gather | bytes 491520 | tf_op jit(solution)/shard_map/while/body/eval_jaxpr/all_gather | solution.py:61
  572.3 34.4 %fusion.24 = f32[16,1536]{1,0:T(8,128)S(1)} fusion(f32[1536,6144]{1,0:T(8,128)} %get-tuple-element.407, f32[2,8,6144]{2,1,0:T(8,128)S(1)} %all_gather.12), kind=kOutput, calls=%fused_computation.2.clone.1 | convolution fusion | flops 1811939328 | bytes 38240256 | tf_op jit(solution)/shard_map/while/body/eval_jaxpr/dot_general | solution.py:16
  606.8 34.6 %fusion.23 = f32[16,1536]{1,0:T(8,128)S(1)} fusion(f32[1536,6144]{1,0:T(8,128)} %get-tuple-element.408, f32[2,8,6144]{2,1,0:T(8,128)S(1)} %all_gather.12), kind=kOutput, calls=%fused_computation.clone.1 | convolution fusion | flops 1811939328 | bytes 38240256 | tf_op jit(solution)/shard_map/while/body/eval_jaxpr/dot_general | solution.py:16
  641.4 1.3 collective-permute-start.1
  642.7 1.3 collective-permute-start
  644.9 7.8 collective-permute-done.1
  653.7 11.8 %all_gather.12 = f32[2,8,6144]{2,1,0:T(8,128)S(1)} all-gather(f32[2,8,1536]{2,1,0:T(8,128)S(1)} %fusion.22), channel_id=1, replica_groups=mesh['sx'=4,'sy'=2,'op'=4] {'op'}, dimensions={2}, use_global_device_ids=true | all-gather | bytes 491520 | tf_op jit(solution)/shard_map/while/body/eval_jaxpr/all_gather | solution.py:61
  665.5 34.4 %fusion.24 = f32[16,1536]{1,0:T(8,128)S(1)} fusion(f32[1536,6144]{1,0:T(8,128)} %get-tuple-element.407, f32[2,8,6144]{2,1,0:T(8,128)S(1)} %all_gather.12), kind=kOutput, calls=%fused_computation.2.clone.1 | convolution fusion | flops 1811939328 | bytes 38240256 | tf_op jit(solution)/shard_map/while/body/eval_jaxpr/dot_general | solution.py:16
  699.9 34.6 %fusion.23 = f32[16,1536]{1,0:T(8,128)S(1)} fusion(f32[1536,6144]{1,0:T(8,128)} %get-tuple-element.408, f32[2,8,6144]{2,1,0:T(8,128)S(1)} %all_gather.12), kind=kOutput, calls=%fused_computation.clone.1 | convolution fusion | flops 1811939328 | bytes 38240256 | tf_op jit(solution)/shard_map/while/body/eval_jaxpr/dot_general | solution.py:16
  734.6 1.3 collective-permute-start.1
  735.9 1.3 collective-permute-start
  738.1 7.8 collective-permute-done.1
  746.8 11.8 %all_gather.12 = f32[2,8,6144]{2,1,0:T(8,128)S(1)} all-gather(f32[2,8,1536]{2,1,0:T(8,128)S(1)} %fusion.22), channel_id=1, replica_groups=mesh['sx'=4,'sy'=2,'op'=4] {'op'}, dimensions={2}, use_global_device_ids=true | all-gather | bytes 491520 | tf_op jit(solution)/shard_map/while/body/eval_jaxpr/all_gather | solution.py:61
  758.6 34.4 %fusion.24 = f32[16,1536]{1,0:T(8,128)S(1)} fusion(f32[1536,6144]{1,0:T(8,128)} %get-tuple-element.407, f32[2,8,6144]{2,1,0:T(8,128)S(1)} %all_gather.12), kind=kOutput, calls=%fused_computation.2.clone.1 | convolution fusion | flops 1811939328 | bytes 38240256 | tf_op jit(solution)/shard_map/while/body/eval_jaxpr/dot_general | solution.py:16
  793.0 34.6 %fusion.23 = f32[16,1536]{1,0:T(8,128)S(1)} fusion(f32[1536,6144]{1,0:T(8,128)} %get-tuple-element.408, f32[2,8,6144]{2,1,0:T(8,128)S(1)} %all_gather.12), kind=kOutput, calls=%fused_computation.clone.1 | convolution fusion | flops 1811939328 | bytes 38240256 | tf_op jit(solution)/shard_map/while/body/eval_jaxpr/dot_general | solution.py:16
  827.7 1.3 collective-permute-start.1
  829.0 1.3 collective-permute-start
  831.2 7.8 collective-permute-done.1
  840.0 11.8 %all_gather.12 = f32[2,8,6144]{2,1,0:T(8,128)S(1)} all-gather(f32[2,8,1536]{2,1,0:T(8,128)S(1)} %fusion.22), channel_id=1, replica_groups=mesh['sx'=4,'sy'=2,'op'=4] {'op'}, dimensions={2}, use_global_device_ids=true | all-gather | bytes 491520 | tf_op jit(solution)/shard_map/while/body/eval_jaxpr/all_gather | solution.py:61
  851.7 34.4 %fusion.24 = f32[16,1536]{1,0:T(8,128)S(1)} fusion(f32[1536,6144]{1,0:T(8,128)} %get-tuple-element.407, f32[2,8,6144]{2,1,0:T(8,128)S(1)} %all_gather.12), kind=kOutput, calls=%fused_computation.2.clone.1 | convolution fusion | flops 1811939328 | bytes 38240256 | tf_op jit(solution)/shard_map/while/body/eval_jaxpr/dot_general | solution.py:16
  886.1 34.6 %fusion.23 = f32[16,1536]{1,0:T(8,128)S(1)} fusion(f32[1536,6144]{1,0:T(8,128)} %get-tuple-element.408, f32[2,8,6144]{2,1,0:T(8,128)S(1)} %all_gather.12), kind=kOutput, calls=%fused_computation.clone.1 | convolution fusion | flops 1811939328 | bytes 38240256 | tf_op jit(solution)/shard_map/while/body/eval_jaxpr/dot_general | solution.py:16
  (81 shorter events, 16.8 us)
Async XLA Ops:
  0.1 3.5 collective-permute-start.1
  1.4 5.4 collective-permute-start
  88.3 7.5 collective-permute-start.1
  89.6 6.3 collective-permute-start
  177.9 10.5 %collective-permute-start.1 = (f32[2,8,1536]{2,1,0:T(8,128)S(1)}, f32[2,8,1536]{2,1,0:T(8,128)S(1)}, u32[]{:S(2)}, u32[]{:S(2)}) collective-permute-start(f32[2,8,1536]{2,1,0:T(8,128)S(1)} %broadcast_select_fusion.2), channel_id=1, source_target_pairs={{0,4},{1,5},{2,6},{3,7},{8,12},{9,13},{10,14},{11,15},{16,20},{17,... | collective-permute-start | bytes 294920 | tf_op jit(solution)/shard_map/while/body/eval_jaxpr/ppermute | solution.py:12
  179.2 9.2 %collective-permute-start = (f32[2,8,1536]{2,1,0:T(8,128)S(1)}, f32[2,8,1536]{2,1,0:T(8,128)S(1)}, u32[]{:S(2)}, u32[]{:S(2)}) collective-permute-start(f32[2,8,1536]{2,1,0:T(8,128)S(1)} %broadcast_select_fusion.2), channel_id=1, source_target_pairs={{0,8},{8,16},{16,24},{1,9},{9,17},{17,25},{2,10},{10,18},{18,26},{... | collective-permute-start | bytes 294920 | tf_op jit(solution)/shard_map/while/body/eval_jaxpr/ppermute | solution.py:12
  270.5 10.6 %collective-permute-start.1 = (f32[2,8,1536]{2,1,0:T(8,128)S(1)}, f32[2,8,1536]{2,1,0:T(8,128)S(1)}, u32[]{:S(2)}, u32[]{:S(2)}) collective-permute-start(f32[2,8,1536]{2,1,0:T(8,128)S(1)} %broadcast_select_fusion.2), channel_id=1, source_target_pairs={{0,4},{1,5},{2,6},{3,7},{8,12},{9,13},{10,14},{11,15},{16,20},{17,... | collective-permute-start | bytes 294920 | tf_op jit(solution)/shard_map/while/body/eval_jaxpr/ppermute | solution.py:12
  271.8 9.3 %collective-permute-start = (f32[2,8,1536]{2,1,0:T(8,128)S(1)}, f32[2,8,1536]{2,1,0:T(8,128)S(1)}, u32[]{:S(2)}, u32[]{:S(2)}) collective-permute-start(f32[2,8,1536]{2,1,0:T(8,128)S(1)} %broadcast_select_fusion.2), channel_id=1, source_target_pairs={{0,8},{8,16},{16,24},{1,9},{9,17},{17,25},{2,10},{10,18},{18,26},{... | collective-permute-start | bytes 294920 | tf_op jit(solution)/shard_map/while/body/eval_jaxpr/ppermute | solution.py:12
  362.9 10.8 %collective-permute-start.1 = (f32[2,8,1536]{2,1,0:T(8,128)S(1)}, f32[2,8,1536]{2,1,0:T(8,128)S(1)}, u32[]{:S(2)}, u32[]{:S(2)}) collective-permute-start(f32[2,8,1536]{2,1,0:T(8,128)S(1)} %broadcast_select_fusion.2), channel_id=1, source_target_pairs={{0,4},{1,5},{2,6},{3,7},{8,12},{9,13},{10,14},{11,15},{16,20},{17,... | collective-permute-start | bytes 294920 | tf_op jit(solution)/shard_map/while/body/eval_jaxpr/ppermute | solution.py:12
  364.2 9.6 %collective-permute-start = (f32[2,8,1536]{2,1,0:T(8,128)S(1)}, f32[2,8,1536]{2,1,0:T(8,128)S(1)}, u32[]{:S(2)}, u32[]{:S(2)}) collective-permute-start(f32[2,8,1536]{2,1,0:T(8,128)S(1)} %broadcast_select_fusion.2), channel_id=1, source_target_pairs={{0,8},{8,16},{16,24},{1,9},{9,17},{17,25},{2,10},{10,18},{18,26},{... | collective-permute-start | bytes 294920 | tf_op jit(solution)/shard_map/while/body/eval_jaxpr/ppermute | solution.py:12
  455.4 11.2 %collective-permute-start.1 = (f32[2,8,1536]{2,1,0:T(8,128)S(1)}, f32[2,8,1536]{2,1,0:T(8,128)S(1)}, u32[]{:S(2)}, u32[]{:S(2)}) collective-permute-start(f32[2,8,1536]{2,1,0:T(8,128)S(1)} %broadcast_select_fusion.2), channel_id=1, source_target_pairs={{0,4},{1,5},{2,6},{3,7},{8,12},{9,13},{10,14},{11,15},{16,20},{17,... | collective-permute-start | bytes 294920 | tf_op jit(solution)/shard_map/while/body/eval_jaxpr/ppermute | solution.py:12
  456.7 9.9 %collective-permute-start = (f32[2,8,1536]{2,1,0:T(8,128)S(1)}, f32[2,8,1536]{2,1,0:T(8,128)S(1)}, u32[]{:S(2)}, u32[]{:S(2)}) collective-permute-start(f32[2,8,1536]{2,1,0:T(8,128)S(1)} %broadcast_select_fusion.2), channel_id=1, source_target_pairs={{0,8},{8,16},{16,24},{1,9},{9,17},{17,25},{2,10},{10,18},{18,26},{... | collective-permute-start | bytes 294920 | tf_op jit(solution)/shard_map/while/body/eval_jaxpr/ppermute | solution.py:12
  548.4 11.2 %collective-permute-start.1 = (f32[2,8,1536]{2,1,0:T(8,128)S(1)}, f32[2,8,1536]{2,1,0:T(8,128)S(1)}, u32[]{:S(2)}, u32[]{:S(2)}) collective-permute-start(f32[2,8,1536]{2,1,0:T(8,128)S(1)} %broadcast_select_fusion.2), channel_id=1, source_target_pairs={{0,4},{1,5},{2,6},{3,7},{8,12},{9,13},{10,14},{11,15},{16,20},{17,... | collective-permute-start | bytes 294920 | tf_op jit(solution)/shard_map/while/body/eval_jaxpr/ppermute | solution.py:12
  549.7 9.9 %collective-permute-start = (f32[2,8,1536]{2,1,0:T(8,128)S(1)}, f32[2,8,1536]{2,1,0:T(8,128)S(1)}, u32[]{:S(2)}, u32[]{:S(2)}) collective-permute-start(f32[2,8,1536]{2,1,0:T(8,128)S(1)} %broadcast_select_fusion.2), channel_id=1, source_target_pairs={{0,8},{8,16},{16,24},{1,9},{9,17},{17,25},{2,10},{10,18},{18,26},{... | collective-permute-start | bytes 294920 | tf_op jit(solution)/shard_map/while/body/eval_jaxpr/ppermute | solution.py:12
  641.4 11.3 %collective-permute-start.1 = (f32[2,8,1536]{2,1,0:T(8,128)S(1)}, f32[2,8,1536]{2,1,0:T(8,128)S(1)}, u32[]{:S(2)}, u32[]{:S(2)}) collective-permute-start(f32[2,8,1536]{2,1,0:T(8,128)S(1)} %broadcast_select_fusion.2), channel_id=1, source_target_pairs={{0,4},{1,5},{2,6},{3,7},{8,12},{9,13},{10,14},{11,15},{16,20},{17,... | collective-permute-start | bytes 294920 | tf_op jit(solution)/shard_map/while/body/eval_jaxpr/ppermute | solution.py:12
  642.7 10.0 %collective-permute-start = (f32[2,8,1536]{2,1,0:T(8,128)S(1)}, f32[2,8,1536]{2,1,0:T(8,128)S(1)}, u32[]{:S(2)}, u32[]{:S(2)}) collective-permute-start(f32[2,8,1536]{2,1,0:T(8,128)S(1)} %broadcast_select_fusion.2), channel_id=1, source_target_pairs={{0,8},{8,16},{16,24},{1,9},{9,17},{17,25},{2,10},{10,18},{18,26},{... | collective-permute-start | bytes 294920 | tf_op jit(solution)/shard_map/while/body/eval_jaxpr/ppermute | solution.py:12
  734.6 11.3 %collective-permute-start.1 = (f32[2,8,1536]{2,1,0:T(8,128)S(1)}, f32[2,8,1536]{2,1,0:T(8,128)S(1)}, u32[]{:S(2)}, u32[]{:S(2)}) collective-permute-start(f32[2,8,1536]{2,1,0:T(8,128)S(1)} %broadcast_select_fusion.2), channel_id=1, source_target_pairs={{0,4},{1,5},{2,6},{3,7},{8,12},{9,13},{10,14},{11,15},{16,20},{17,... | collective-permute-start | bytes 294920 | tf_op jit(solution)/shard_map/while/body/eval_jaxpr/ppermute | solution.py:12
  735.9 10.0 %collective-permute-start = (f32[2,8,1536]{2,1,0:T(8,128)S(1)}, f32[2,8,1536]{2,1,0:T(8,128)S(1)}, u32[]{:S(2)}, u32[]{:S(2)}) collective-permute-start(f32[2,8,1536]{2,1,0:T(8,128)S(1)} %broadcast_select_fusion.2), channel_id=1, source_target_pairs={{0,8},{8,16},{16,24},{1,9},{9,17},{17,25},{2,10},{10,18},{18,26},{... | collective-permute-start | bytes 294920 | tf_op jit(solution)/shard_map/while/body/eval_jaxpr/ppermute | solution.py:12
  827.7 11.3 %collective-permute-start.1 = (f32[2,8,1536]{2,1,0:T(8,128)S(1)}, f32[2,8,1536]{2,1,0:T(8,128)S(1)}, u32[]{:S(2)}, u32[]{:S(2)}) collective-permute-start(f32[2,8,1536]{2,1,0:T(8,128)S(1)} %broadcast_select_fusion.2), channel_id=1, source_target_pairs={{0,4},{1,5},{2,6},{3,7},{8,12},{9,13},{10,14},{11,15},{16,20},{17,... | collective-permute-start | bytes 294920 | tf_op jit(solution)/shard_map/while/body/eval_jaxpr/ppermute | solution.py:12
  829.0 10.0 %collective-permute-start = (f32[2,8,1536]{2,1,0:T(8,128)S(1)}, f32[2,8,1536]{2,1,0:T(8,128)S(1)}, u32[]{:S(2)}, u32[]{:S(2)}) collective-permute-start(f32[2,8,1536]{2,1,0:T(8,128)S(1)} %broadcast_select_fusion.2), channel_id=1, source_target_pairs={{0,8},{8,16},{16,24},{1,9},{9,17},{17,25},{2,10},{10,18},{18,26},{... | collective-permute-start | bytes 294920 | tf_op jit(solution)/shard_map/while/body/eval_jaxpr/ppermute | solution.py:12
  920.8 0.7 copy-start
where the time goes:
time: 935 us; the launch traced here: 921 us
  matrix products  690 us (74%)
  blocking collectives  118 us (13%)
  waiting for transfers between devices  67.3 us (7%)
  starting transfers between devices  25.8 us (3%)
  other arithmetic  10.3 us (1%)
    dot_general x20, matrix products, contract(): lax.dot_general(left, right, (((1,), (1,)), ((), ())), precision=lax.Prec...  690 us
    all_gather x10, blocking collectives, section(): result = accumulate(lax.all_gather(incoming, 'op', axis=2, tiled=True))  118 us
    ppermute x20, waiting for transfers between devices, from_behind(): return lax.ppermute(value, axis, pairs)  67.3 us
    ppermute x20, starting transfers between devices, from_behind(): return lax.ppermute(value, axis, pairs)  25.8 us
  transfers between devices with their start and end apart: 20, of which 10 were waited for; matrix products, arithmetic and copies ran while one was open for 1% of the time, Pallas kernels for 0%

commit v1 on v0

v1 whole, which is shorter than its diff:
```python
import functools

import jax
import jax.numpy as jnp
from jax import lax
from jax.experimental import pallas as pl
from jax.experimental.pallas import tpu as pltpu
from jax.sharding import PartitionSpec as P

MESH = pl.DeviceIdType.MESH
LOAD_ROWS = 32
SLOTS = 3
LOW_SCALE = 2.0**20
F8 = jnp.float8_e4m3fn
F32 = jnp.float32
BF16 = jnp.bfloat16
NT = (((1,), (1,)), ((), ()))


def kernel(
    ncol, nrow, nop, groups, block,
    real_hbm, imag_hbm, right_ref, upper_ref, src_ref, out_ref,
    high, low, stage, gathered, xw, x8, inv, left_buf, below_buf, trace,
    load_sem, gsend, grecv, lsend, lrecv, usend, urecv,
):
    c = lax.axis_index("sx")
    r = lax.axis_index("sy")
    z = lax.axis_index("op")
    first = c + r == 0
    rows, width = real_hbm.shape
    srcs = src_ref.shape[1]
    group_rows = rows // groups
    chunks = rows // LOAD_ROWS
    per_block = block // LOAD_ROWS
    blocks = group_rows // block
    ops = (real_hbm, imag_hbm)

    def load(chunk, slot, k):
        at = pl.multiple_of(chunk * LOAD_ROWS, LOAD_ROWS)
        return pltpu.make_async_copy(
            ops[k].at[pl.ds(at, LOAD_ROWS), :], stage.at[slot, k], load_sem.at[slot, k]
        )

    for s in range(SLOTS):
        for k in range(2):
            load(s, s, k).start()

    barrier = pltpu.get_barrier_semaphore()
    for j in range(1, nop):
        pl.semaphore_signal(
            barrier, inc=1, device_id=(c, r, lax.rem(z + j, nop)), device_id_type=MESH
        )

    def greet(cond, cc, rr):
        @pl.when(cond)
        def _():
            pl.semaphore_signal(barrier, inc=1, device_id=(cc, rr, z), device_id_type=MESH)

    has_left, has_right = c > 0, c < ncol - 1
    has_below, has_above = r > 0, r < nrow - 1
    greet(has_left, c - 1, r)
    greet(has_right, c + 1, r)
    greet(has_below, c, r - 1)
    greet(has_above, c, r + 1)
    near = sum(jnp.where(cond, 1, 0) for cond in (has_left, has_right, has_below, has_above))
    pl.semaphore_wait(barrier, nop - 1 + near)

    def send_right(g):
        return pltpu.make_async_remote_copy(
            trace.at[g], left_buf.at[g], lsend.at[g], lrecv.at[g],
            device_id=(c + 1, r, z), device_id_type=MESH,
        )

    def send_up(g):
        return pltpu.make_async_remote_copy(
            trace.at[g], below_buf.at[g], usend.at[g], urecv.at[g],
            device_id=(c, r + 1, z), device_id_type=MESH,
        )

    def share(g, j):
        peer = lax.rem(z + j, nop)
        return pltpu.make_async_remote_copy(
            gathered.at[z, g], gathered.at[z, g], gsend.at[g, j], grecv.at[g, j],
            device_id=(c, r, peer), device_id_type=MESH,
        )

    def gather():
        for g in range(groups):
            cols = pl.ds(g * group_rows, group_rows)
            gathered[z, g] = src_ref[:, :, cols]

            def add(coef_ref, buf):
                cr = coef_ref[0:1, cols]
                ci = coef_ref[1:2, cols]
                gathered[z, g, 0] += cr * buf[g, 0] - ci * buf[g, 1]
                gathered[z, g, 1] += cr * buf[g, 1] + ci * buf[g, 0]

            @pl.when(has_left)
            def _():
                send_right(g).wait_recv()
                add(right_ref, left_buf)

            @pl.when(has_below)
            def _():
                send_up(g).wait_recv()
                add(upper_ref, below_buf)

            for j in range(1, nop):
                share(g, j).start()
        for g in range(groups):
            for j in range(1, nop):
                share(g, j).wait()

        def largest(step, top):
            zz, g = step // groups, lax.rem(step, groups)
            both = jnp.maximum(jnp.abs(gathered[zz, g, 0]), jnp.abs(gathered[zz, g, 1]))
            return jnp.maximum(top, jnp.max(both, axis=1, keepdims=True))

        top = lax.fori_loop(0, nop * groups, largest, jnp.zeros((srcs, 1), F32))
        top = jnp.maximum(top, 1e-30)
        inv[...] = jnp.broadcast_to(top * (1.0 / (256.0 * LOW_SCALE)), inv.shape)
        scale = 256.0 / top

        @pl.loop(0, nop * groups)
        def _(step):
            zz, g = step // groups, lax.rem(step, groups)
            at = pl.multiple_of(step * group_rows, group_rows)
            for k in range(2):
                value = gathered[zz, g, k]
                top_part = value.astype(BF16)
                xw[k * srcs:(k + 1) * srcs, pl.ds(at, group_rows)] = top_part
                xw[(2 + k) * srcs:(3 + k) * srcs, pl.ds(at, group_rows)] = (
                    value - top_part.astype(F32)
                ).astype(BF16)
            both = jnp.concatenate([gathered[zz, g, 0] * scale, gathered[zz, g, 1] * scale], axis=0)
            x8[:, pl.ds(at, group_rows)] = both.astype(F8)

    def convert(b):
        @pl.loop(0, per_block)
        def _(i):
            chunk = b * per_block + i
            slot = lax.rem(chunk, SLOTS)
            at = pl.multiple_of(chunk * LOAD_ROWS, LOAD_ROWS)
            for k in range(2):
                load(chunk, slot, k).wait()

                @pl.loop(0, width // 512)
                def _(q):
                    cols = pl.ds(pl.multiple_of(q * 512, 512), 512)
                    value = stage[slot, k, :, cols]
                    top_part = value.astype(BF16)
                    high[k, pl.ds(at, LOAD_ROWS), cols] = top_part
                    low[k, pl.ds(at, LOAD_ROWS), cols] = (
                        (value - top_part.astype(F32)) * LOW_SCALE
                    ).astype(F8)

            @pl.when(chunk + SLOTS < chunks)
            def _():
                for k in range(2):
                    load(chunk + SLOTS, slot, k).start()

    def multiply(g, b):
        at = pl.ds(pl.multiple_of((g * blocks + b) * block, block), block)
        here = pl.ds(pl.multiple_of(b * block, block), block)
        parts = []
        for k in range(2):
            big = lax.dot_general(xw[...], high[k, at, :], NT, preferred_element_type=F32)
            small = lax.dot_general(x8[...], low[k, at, :], NT, preferred_element_type=F32)
            factor = jnp.concatenate([inv[:, :1], inv[:, :1]], axis=0)
            parts.append(big[:2 * srcs] + (big[2 * srcs:] + small * factor))
        trace[g, 0, :, here] = parts[0][:srcs] - parts[1][srcs:]
        trace[g, 1, :, here] = parts[1][:srcs] + parts[0][srcs:]

    def publish(g):
        @pl.when(has_right)
        def _():
            send_right(g).start()

        @pl.when(has_above)
        def _():
            send_up(g).start()

        out_ref[:, :, g * group_rows:(g + 1) * group_rows] = trace[g]

    @pl.when(first)
    def _():
        gather()

    for phase in range(2):
        @pl.when(True if phase == 0 else jnp.logical_not(first))
        def _():
            if phase == 1:
                gather()
            for g in range(groups):
                @pl.loop(0, blocks)
                def _(b):
                    if phase == 0:
                        convert(g * blocks + b)

                        @pl.when(first)
                        def _():
                            multiply(g, b)
                    else:
                        multiply(g, b)
                if phase == 0:
                    @pl.when(first)
                    def _():
                        publish(g)
                else:
                    publish(g)

    for g in range(groups):
        @pl.when(has_right)
        def _():
            send_right(g).wait_send()

        @pl.when(has_above)
        def _():
            send_up(g).wait_send()


def solution(mesh):
    ncol, nrow, nop = (mesh.shape[a] for a in ("sx", "sy", "op"))

    def shards(op_real, op_imag, coef_right, coef_upper, sources):
        rows, width = op_real.shape[2:]
        srcs = sources.shape[3]
        groups = 3 if rows % 384 == 0 else 1
        group_rows = rows // groups
        block = 256 if group_rows % 256 == 0 else 128
        vmem = pl.BlockSpec(memory_space=pltpu.VMEM)
        hbm = pl.BlockSpec(memory_space=pl.ANY)
        dma = pltpu.SemaphoreType.DMA
        out = pl.pallas_call(
            functools.partial(kernel, ncol, nrow, nop, groups, block),
            out_shape=jax.ShapeDtypeStruct((2, srcs, rows), F32),
            in_specs=[hbm, hbm, vmem, vmem, vmem],
            out_specs=vmem,
            scratch_shapes=[
                pltpu.VMEM((2, rows, width), BF16),
                pltpu.VMEM((2, rows, width), F8),
                pltpu.VMEM((SLOTS, 2, LOAD_ROWS, width), F32),
                pltpu.VMEM((nop, groups, 2, srcs, group_rows), F32),
                pltpu.VMEM((4 * srcs, width), BF16),
                pltpu.VMEM((2 * srcs, width), F8),
                pltpu.VMEM((srcs, 128), F32),
                pltpu.VMEM((groups, 2, srcs, group_rows), F32),
                pltpu.VMEM((groups, 2, srcs, group_rows), F32),
                pltpu.VMEM((groups, 2, srcs, group_rows), F32),
                dma((SLOTS, 2)),
                dma((groups, nop)),
                dma((groups, nop)),
                dma((groups,)),
                dma((groups,)),
                dma((groups,)),
                dma((groups,)),
            ],
            compiler_params=pltpu.CompilerParams(
                collective_id=0, has_side_effects=True, vmem_limit_bytes=67043328
            ),
        )(op_real[0, 0], op_imag[0, 0], coef_right[0, 0], coef_upper[0, 0], sources[0, 0])
        return out[None, None]

    return jax.shard_map(
        shards,
        mesh=mesh,
        in_specs=(
            P("sx", "sy", "op", None),
            P("sx", "sy", "op", None),
            P("sx", "sy", None, "op"),
            P("sx", "sy", None, "op"),
            P("sx", "sy", None, None, "op"),
        ),
        out_specs=P("sx", "sy", None, None, "op"),
        check_vma=False,
    )
```

time: 935 us -> 164 us (0.18); the launches traced: 921 us -> 164 us
  matrix products: 690 us -> 0 us
  Pallas kernels: 0 us -> 162 us
  blocking collectives: 118 us -> 0 us
  waiting for transfers between devices: 67.3 us -> 0 us
  starting transfers between devices: 25.8 us -> 0 us
  other arithmetic: 10.3 us -> 0 us
    dot_general x20 -> x0, matrix products: 690 us -> none  [contract(): lax.dot_general(left, right, (((1,), (1,)), ((), ())), precision=lax.Prec...]
    pallas_call x0 -> x1, Pallas kernels: none -> 162 us  [shards(): pl.pallas_call(functools.partial(kernel, ncol, nrow, nop, groups, block),...]
    all_gather x10 -> x0, blocking collectives: 118 us -> none  [section(): result = accumulate(lax.all_gather(incoming, 'op', axis=2, tiled=True))]
    ppermute x20 -> x0, waiting for transfers between devices: 67.3 us -> none  [from_behind(): return lax.ppermute(value, axis, pairs)]
    ppermute x20 -> x0, starting transfers between devices: 25.8 us -> none  [from_behind(): return lax.ppermute(value, axis, pairs)]
  transfers between devices with their start and end apart: 20 -> 0, of which waited for: 10 -> 0; matrix products, arithmetic and copies ran while one was open for 1% -> 0% of each run, Pallas kernels for 0% -> 0%
where the time goes in v1:
time: 164 us
  Pallas kernels  162 us (99%)
    pallas_call x1, Pallas kernels, shards(): pl.pallas_call(functools.partial(kernel, ncol, nrow, nop, groups, block),...  162 us

profile of v1, /device:TPU:7, one launch (start us, length us, event | category | flops | bytes accessed | tf_op | source)
XLA Modules:
  0.0 163.8 jit_solution(11511976823918958952)
XLA Ops:
  0.0 162.2 %shard_map.55 = f32[2,16,1536]{2,1,0:T(8,128)} custom-call(f32[1536,6144]{1,0:T(8,128)} %bitcast.6, f32[1536,6144]{1,0:T(8,128)} %bitcast.7, f32[2,1536]{1,0:T(2,128)} %bitcast.10, f32[2,1536]{1,0:T(2,128)} %bitcast.11, f32[2,16,1536]{2,1,0:T(8,128)} %bitcast.9), custom_call_target="tpu_custom_call" | custom-call | tf_op jit(solution)/shard_map/pallas_call | solution.py:234
  162.2 1.6 copy.7
